TPU v7x, 32 devices: a whole 2x2x4 slice. The times are simulated.
32 devices in a mesh: band: 4 (over y, x), cell: 8 (over z, core).
Axes of the slice: x: 2, y: 2, z: 4, core: 2. Of those that a mesh axis runs over, the one named last changes fastest.
Arguments:
- wavefunctions: bfloat16 [512, 28672], P('band', 'cell'), may hold values from -24 to 24
- stiffness: bfloat16 [512, 512], replicated, may hold values from -1 to 2
- cell_scale: float32 [64], P('cell'), may hold values from 0.5 to 1.5
- potential: float32 [64, 512], P('cell'), may hold values from 0 to 1
Outputs:
- rotated: bfloat16 [512, 28672], P('band', 'cell')
All inputs are finite; a program needn't handle non-finite values.
Results may differ from a plain program's by a relative error of at most 0.0022.
The roundings to bfloat16 on the way count: a program that leaves them out, or rounds other values in their place, can miss the bound.
Values may be sent and summed in bfloat16 or wider, within the bound.
A program may use at most 64 MiB of HBM per device.

v0:
```python
import functools
import jax
import jax.numpy as jnp
from jax import lax
from jax.experimental import pallas as pl
from jax.experimental.pallas import tpu as pltpu
from jax.sharding import PartitionSpec as P

PLANE = 64
OWN = 448
BLK = 128
PAN = 8
MESH = pl.DeviceIdType.MESH

centre = 4.0
half_width = 3.0


def shifted(block, axis, distance):
    devices = range(lax.axis_size(axis))
    route = [((i - distance) % len(devices), i) for i in devices]
    return lax.ppermute(block, axis, route)


def apply_h(field, stiffness, cell_scale, potential):
    band_rows = field.shape[0]
    cell_count = field.shape[1] // OWN
    following = shifted(field[:, :PLANE], "cell", -1)
    owned_part = field.reshape(band_rows, cell_count, OWN)
    top_plane = jnp.concatenate([owned_part[:, 1:, :PLANE], following[:, None, :]], 1)
    cell_nodes = jnp.concatenate([owned_part, top_plane], 2)
    stiff_part = jnp.einsum(
        "bcn,nm->bcm", cell_nodes, stiffness, preferred_element_type=jnp.float32
    )
    cell_result = cell_scale[None, :, None] * stiff_part + potential[None] * cell_nodes.astype(
        jnp.float32
    )
    spill = cell_result[:, :, OWN:]
    incoming = shifted(spill[:, -1], "cell", 1)
    spill = jnp.concatenate([incoming[:, None, :], spill[:, :-1]], 1)
    kept = cell_result[:, :, :OWN]
    kept = jnp.concatenate([kept[:, :, :PLANE] + spill, kept[:, :, PLANE:]], 2)
    return kept.reshape(band_rows, cell_count * OWN)


def place(i, j, count):
    if i >= count // 2:
        return (count - 1 - i) * BLK, j * BLK
    return i * BLK, (count - i + j) * BLK


def packed_gram(slices_ref, packed_ref, count):
    for i in range(count):
        row, col = place(i, 0, count)
        width = (i + 1) * BLK
        packed_ref[row : row + BLK, col : col + width] = lax.dot_general(
            slices_ref[i * BLK : (i + 1) * BLK, :],
            slices_ref[:width, :],
            (((1,), (1,)), ((), ())),
            preferred_element_type=jnp.float32,
        )


def gram_kernel(count, slices_ref, packed_ref):
    packed_gram(slices_ref, packed_ref, count)


def reduce_kernel(
    count, bands, cells, total,
    slices_ref, out_ref,
    mine, from_core, half, from_band, quarter, from_z, piece,
    send_sem, recv_sem,
):
    band = lax.axis_index("band")
    cell = lax.axis_index("cell")
    core = lax.rem(cell, 2)
    level = lax.div(cell, 2)
    levels = cells // 2
    rows_half = mine.shape[0] // 2
    rows_band = rows_half // bands
    rows_z = rows_band // levels

    other_core = {"band": band, "cell": cell + 1 - 2 * core}
    band_peer = lambda o: lax.rem(band + o, bands)
    z_peer = lambda o: lax.rem(level + o, levels)
    band_device = lambda o: {"band": band_peer(o), "cell": cell}
    z_device = lambda o: {"band": band, "cell": z_peer(o) * 2 + core}

    barrier = pltpu.get_barrier_semaphore()
    pl.semaphore_signal(barrier, inc=1, device_id=other_core, device_id_type=MESH)
    for o in range(1, bands):
        pl.semaphore_signal(barrier, inc=1, device_id=band_device(o), device_id_type=MESH)
    for o in range(1, levels):
        pl.semaphore_signal(barrier, inc=1, device_id=z_device(o), device_id_type=MESH)

    packed_gram(slices_ref, mine, count)
    pl.semaphore_wait(barrier, 1 + (bands - 1) + (levels - 1))

    used = [0]

    def send(src, dst, device):
        slot = used[0]
        used[0] += 1
        copy = pltpu.make_async_remote_copy(
            src_ref=src, dst_ref=dst, send_sem=send_sem.at[slot], recv_sem=recv_sem.at[slot],
            device_id=device, device_id_type=MESH,
        )
        copy.start()
        return copy

    def rows(start, size):
        return pl.ds(pl.multiple_of(start, 8), size)

    copy = send(mine.at[rows((1 - core) * rows_half, rows_half)], from_core, other_core)
    copy.wait()
    half[...] = mine[rows(core * rows_half, rows_half), :] + from_core[...]

    copies = [
        send(half.at[rows(band_peer(o) * rows_band, rows_band)], from_band.at[o - 1], band_device(o))
        for o in range(1, bands)
    ]
    for copy in copies:
        copy.wait()
    summed = half[rows(band * rows_band, rows_band), :]
    for o in range(1, bands):
        summed = summed + from_band[o - 1]
    quarter[...] = summed

    copies = [
        send(quarter.at[rows(z_peer(o) * rows_z, rows_z)], from_z.at[o - 1], z_device(o))
        for o in range(1, levels)
    ]
    for copy in copies:
        copy.wait()
    summed = quarter[rows(level * rows_z, rows_z), :]
    for o in range(1, levels):
        summed = summed + from_z[o - 1]
    summed = summed / total
    piece[...] = summed

    start_half = core * rows_half
    start_band = start_half + band * rows_band
    start_z = start_band + level * rows_z
    here = rows(start_z, rows_z)
    out_ref[here, :] = summed
    copies = [send(piece, out_ref.at[here], z_device(o)) for o in range(1, levels)]
    for copy in copies:
        copy.wait()
    here = out_ref.at[rows(start_band, rows_band)]
    copies = [send(here, here, band_device(o)) for o in range(1, bands)]
    for copy in copies:
        copy.wait()
    here = out_ref.at[rows(start_half, rows_half)]
    send(here, here, other_core).wait()


def margin_packed(slices):
    bands, cells = lax.axis_size("band"), lax.axis_size("cell")
    band_total, nodes = slices.shape
    count = band_total // BLK
    total = float(nodes * bands * cells)
    height, width = band_total // 2, (count + 1) * BLK
    shape = jax.ShapeDtypeStruct((height, width), jnp.float32)
    vmem = pl.BlockSpec(memory_space=pltpu.VMEM)
    if cells % 2 or cells < 4 or bands < 2 or height % (8 * bands * cells):
        partial = pl.pallas_call(
            functools.partial(gram_kernel, count), out_shape=shape, in_specs=[vmem], out_specs=vmem
        )(slices)
        return lax.psum(partial, ("band", "cell")) / total
    levels = cells // 2
    rows_half = height // 2
    rows_band = rows_half // bands
    rows_z = rows_band // levels
    sends = 2 * (1 + (bands - 1) + (levels - 1))
    f32 = jnp.float32
    return pl.pallas_call(
        functools.partial(reduce_kernel, count, bands, cells, total),
        out_shape=shape,
        in_specs=[vmem],
        out_specs=vmem,
        scratch_shapes=[
            pltpu.VMEM((height, width), f32),
            pltpu.VMEM((rows_half, width), f32),
            pltpu.VMEM((rows_half, width), f32),
            pltpu.VMEM((bands - 1, rows_band, width), f32),
            pltpu.VMEM((rows_band, width), f32),
            pltpu.VMEM((levels - 1, rows_z, width), f32),
            pltpu.VMEM((rows_z, width), f32),
            pltpu.SemaphoreType.DMA((sends,)),
            pltpu.SemaphoreType.DMA((sends,)),
        ],
        compiler_params=pltpu.CompilerParams(collective_id=0, has_side_effects=True),
    )(slices)


def invert_block(block_ref):
    tiles = BLK // PAN
    shape = (PAN, BLK)
    lane = lax.broadcasted_iota(jnp.int32, shape, 1)
    row = lax.broadcasted_iota(jnp.int32, shape, 0)
    left = [block_ref[t * PAN : (t + 1) * PAN, :] for t in range(tiles)]
    right = [jnp.where(lane == row + t * PAN, 1.0, 0.0).astype(jnp.float32) for t in range(tiles)]

    def spread(value):
        return jnp.broadcast_to(value, shape)

    for m in range(tiles):
        k = m * PAN
        grid = {
            (i, j): spread(left[m][i : i + 1, k + j : k + j + 1])
            for j in range(PAN)
            for i in range(j, PAN)
        }
        cols = [
            [spread(left[t][:, k + j : k + j + 1]) for t in range(m + 1, tiles)] for j in range(PAN)
        ]
        rows_left = [spread(left[m][j : j + 1, :]) for j in range(PAN)]
        rows_right = [spread(right[m][j : j + 1, :]) for j in range(PAN)]
        for j in range(PAN):
            scale = lax.rsqrt(grid[j, j])
            rows_left[j] = rows_left[j] * scale
            rows_right[j] = rows_right[j] * scale
            cols[j] = [c * scale for c in cols[j]]
            factor = {i: grid[i, j] * scale for i in range(j + 1, PAN)}
            for i in range(j + 1, PAN):
                for q in range(j + 1, i + 1):
                    grid[i, q] = grid[i, q] - factor[i] * factor[q]
                rows_left[i] = rows_left[i] - factor[i] * rows_left[j]
                rows_right[i] = rows_right[i] - factor[i] * rows_right[j]
                cols[i] = [c - factor[i] * d for c, d in zip(cols[i], cols[j])]
        for n, t in enumerate(range(m + 1, tiles)):
            for j in range(PAN):
                left[t] = left[t] - cols[j][n] * rows_left[j]
                right[t] = right[t] - cols[j][n] * rows_right[j]
        done = rows_right[0]
        for j in range(1, PAN):
            done = jnp.where(row == j, rows_right[j], done)
        right[m] = done
    return right


def exact(a, b, dims):
    return lax.dot_general(
        a, b, (dims, ((), ())), precision=lax.Precision.HIGHEST, preferred_element_type=jnp.float32
    )


NN = ((1,), (0,))
NT = ((1,), (1,))


def factor_kernel(count, packed_ref, out_ref, work, lower, inv, diag):
    size = count * BLK
    for i in range(count):
        row, col = place(i, 0, count)
        width = (i + 1) * BLK
        work[i * BLK : (i + 1) * BLK, :width] = packed_ref[row : row + BLK, col : col + width]
    inv[...] = jnp.zeros_like(inv)
    diag[...] = work[:BLK, :BLK]

    @pl.loop(0, count)
    def _(step):
        tiles = invert_block(diag)
        for t, tile in enumerate(tiles):
            diag[t * PAN : (t + 1) * PAN, :] = tile
        for j in range(count):

            @pl.when(step == j)
            def _():
                here = slice(j * BLK, (j + 1) * BLK)
                top = diag[...]
                if j:
                    partial = exact(lower[here, : j * BLK], inv[: j * BLK, : j * BLK], NN)
                    inv[here, : j * BLK] = -exact(top, partial, NN)
                inv[here, here] = top
                if j + 1 < count:
                    below = slice((j + 1) * BLK, size)
                    panel = exact(work[below, here], top, NT)
                    lower[below, here] = panel
                    work[below, below] = work[below, below] - exact(panel, panel, NT)
                    diag[...] = work[(j + 1) * BLK : (j + 2) * BLK, (j + 1) * BLK : (j + 2) * BLK]

    out_ref[...] = inv[...].astype(out_ref.dtype)


def inverse_factor(packed):
    size = packed.shape[0] * 2
    count = size // BLK
    vmem = pl.BlockSpec(memory_space=pltpu.VMEM)
    return pl.pallas_call(
        functools.partial(factor_kernel, count),
        out_shape=jax.ShapeDtypeStruct((size, size), jnp.bfloat16),
        in_specs=[vmem],
        out_specs=vmem,
        scratch_shapes=[
            pltpu.VMEM((size, size), jnp.float32),
            pltpu.VMEM((size, size), jnp.float32),
            pltpu.VMEM((size, size), jnp.float32),
            pltpu.VMEM((BLK, BLK), jnp.float32),
        ],
    )(packed)


def shards(wavefunctions, stiffness, cell_scale, potential):
    anchor = wavefunctions.astype(jnp.float32)
    degree_one = (
        (apply_h(wavefunctions, stiffness, cell_scale, potential) - centre * anchor) / half_width
    ).astype(jnp.bfloat16)
    one_wide = degree_one.astype(jnp.float32)
    degree_two = (
        2.0
        * (apply_h(degree_one, stiffness, cell_scale, potential) - centre * one_wide)
        / half_width
        - anchor
    ).astype(jnp.bfloat16)
    two_wide = degree_two.astype(jnp.float32)
    degree_three = (
        2.0
        * (apply_h(degree_two, stiffness, cell_scale, potential) - centre * two_wide)
        / half_width
        - one_wide
    ).astype(jnp.bfloat16)
    slices = lax.all_to_all(degree_three, "band", split_axis=1, concat_axis=0, tiled=True)
    inverse = inverse_factor(margin_packed(slices))
    rotated = jnp.dot(inverse, slices, preferred_element_type=jnp.float32).astype(jnp.bfloat16)
    return lax.all_to_all(rotated, "band", split_axis=0, concat_axis=1, tiled=True)


def solution(mesh):
    in_specs = (P("band", "cell"), P(), P("cell"), P("cell", None))
    out_specs = P("band", "cell")
    return jax.shard_map(shards, mesh=mesh, in_specs=in_specs, out_specs=out_specs, check_vma=False)
```

profile of v0, /device:TPU:0, one launch (start us, length us, event | category | flops | bytes accessed | tf_op | source)
XLA Modules:
  0.0 142.4 jit_solution(5619424418631946339)
XLA Ops:
  0.0 0.8 slice.73
  0.8 4.5 %collective-permute-start = (bf16[128,64]{1,0:T(8,128)(2,1)S(1)}, bf16[128,64]{1,0:T(8,128)(2,1)S(1)}, u32[]{:S(2)}, u32[]{:S(2)}) collective-permute-start(bf16[128,64]{1,0:T(8,128)(2,1)S(1)} %slice.73), channel_id=1, source_target_pairs={{1,0},{2,1},{3,2},{4,3},{5,4},{6,5},{7,6},{0,7},{9,8},{10,9},{11,1... | collective-permute-start | bytes 49160 | tf_op jit(solution)/shard_map/ppermute | solution.py:22
  5.3 1.5 %copy.12 = bf16[128,3584]{0,1:T(8,128)(2,1)S(1)} copy(bf16[128,3584]{1,0:T(8,128)(2,1)} %param.4) | data formatting | bytes 1835008 | tf_op args[0]
  6.9 0.5 copy.14
  7.5 0.7 multiply_add_fusion.2
  8.3 0.1 slice_bitcast_fusion.2
  8.4 0.2 slice.93
  8.6 0.5 slice.94
  9.1 4.8 %collective-permute-done.1 = f32[128,64]{1,0:T(8,128)S(1)} collective-permute-done((f32[128,64]{1,0:T(8,128)S(1)}, f32[128,64]{1,0:T(8,128)S(1)}, u32[]{:S(2)}, u32[]{:S(2)}) %collective-permute-start.1) | collective-permute-done | bytes 32800 | tf_op jit(solution)/shard_map/ppermute | solution.py:22
  13.9 0.1 slice_add_fusion.2
  14.0 0.6 pad_maximum_fusion
  14.6 1.8 %copy.15 = f32[128,8,448]{0,2,1:T(8,128)} copy(f32[128,8,448]{2,0,1:T(8,128)S(1)} %pad_maximum_fusion) | data formatting | bytes 3670016 | tf_op jit(solution)/shard_map/concatenate | solution.py:42
  16.4 2.8 %copy.16 = f32[128,3584]{1,0:T(8,128)} copy(f32[128,3584]{0,1:T(8,128)} %bitcast.38) | data formatting | bytes 3670016 | tf_op jit(solution)/shard_map/reshape | solution.py:43
  19.2 1.8 %fusion.2 = bf16[128,3584]{1,0:T(8,128)(2,1)S(1)} fusion(f32[128,3584]{1,0:T(8,128)} %copy.16, bf16[128,3584]{1,0:T(8,128)(2,1)S(1)} %copy-done.1), kind=kLoop, calls=%fused_computation.12 | loop fusion | flops 2293760 | bytes 3670016 | tf_op jit(solution)/shard_map/convert_element_type | solution.py:308
  21.1 0.6 copy.17
  21.7 1.3 copy.19
  23.0 1.0 slice.95
  24.0 2.3 %multiply_add_fusion.1 = f32[128,8,512]{2,0,1:T(8,128)S(1)} fusion(bf16[128,1,64]{2,0,1:T(8,128)(2,1)S(1)} %bitcast.54, bf16[128,7,64]{2,0,1:T(8,128)(2,1)S(1)} %slice.95, bf16[128,8,448]{2,0,1:T(8,128)(2,1)} %copy.19, f32[8,512]{1,0:T(8,128)S(1)} %copy-done.3, f32[8]{0:T(128)S(1)} %copy-done.5, bf16[512,512]{1,0:T(8,128)(2,1)S(1)} %copy-done), kind=kOutput, calls=%fused_computation.8 | convolution fusion | flops 544735232 | bytes 3686432 | tf_op jit(solution)/shard_map/bcn,nm->bcm/dot_general | solution.py:32
  26.3 0.1 slice_bitcast_fusion.1
  26.4 0.5 collective-permute-start.3
  26.9 0.2 slice.99
  27.1 0.5 slice.100
  27.6 4.3 %collective-permute-done.3 = f32[128,64]{1,0:T(8,128)S(1)} collective-permute-done((f32[128,64]{1,0:T(8,128)S(1)}, f32[128,64]{1,0:T(8,128)S(1)}, u32[]{:S(2)}, u32[]{:S(2)}) %collective-permute-start.3) | collective-permute-done | bytes 32800 | tf_op jit(solution)/shard_map/ppermute | solution.py:22
  31.9 0.1 slice_add_fusion.1
  32.0 1.9 %pad_maximum_fusion.1 = f32[128,8,448]{2,0,1:T(8,128)} fusion(f32[128,8,384]{2,0,1:T(8,128)S(1)} %slice.100, f32[128,8,64]{2,0,1:T(8,128)S(1)} %slice_add_fusion.1), kind=kLoop, calls=%fused_computation.5 | loop fusion | flops 458752 | bytes 3670016 | tf_op jit(solution)/shard_map/concatenate | solution.py:42
  33.9 2.8 %copy.20 = f32[128,8,448]{0,2,1:T(8,128)} copy(f32[128,8,448]{2,0,1:T(8,128)} %pad_maximum_fusion.1) | data formatting | bytes 3670016 | tf_op jit(solution)/shard_map/concatenate | solution.py:42
  36.8 2.8 %copy.21 = f32[128,3584]{1,0:T(8,128)} copy(f32[128,3584]{0,1:T(8,128)} %bitcast.39) | data formatting | bytes 3670016 | tf_op jit(solution)/shard_map/reshape | solution.py:43
  39.5 1.9 %fusion.3 = bf16[128,3584]{1,0:T(8,128)(2,1)S(1)} fusion(bf16[128,3584]{1,0:T(8,128)(2,1)S(1)} %copy-done.1, f32[128,3584]{1,0:T(8,128)} %copy.21, bf16[128,3584]{1,0:T(8,128)(2,1)S(1)} %fusion.2), kind=kLoop, calls=%fused_computation.13 | loop fusion | flops 3211264 | bytes 4587520 | tf_op jit(solution)/shard_map/convert_element_type | solution.py:315
  41.5 0.6 copy.22
  42.1 1.3 copy.24
  43.4 1.0 slice.101
  44.4 2.3 %multiply_add_fusion = f32[128,8,512]{2,0,1:T(8,128)S(1)} fusion(bf16[128,1,64]{2,0,1:T(8,128)(2,1)S(1)} %bitcast.55, bf16[128,7,64]{2,0,1:T(8,128)(2,1)S(1)} %slice.101, bf16[128,8,448]{2,0,1:T(8,128)(2,1)} %copy.24, f32[8,512]{1,0:T(8,128)S(1)} %copy-done.3, f32[8]{0:T(128)S(1)} %copy-done.5, bf16[512,512]{1,0:T(8,128)(2,1)S(1)} %copy-done), kind=kOutput, calls=%fused_computation.7 | convolution fusion | flops 544735232 | bytes 3686432 | tf_op jit(solution)/shard_map/bcn,nm->bcm/dot_general | solution.py:32
  46.7 0.1 slice_bitcast_fusion
  46.8 0.5 collective-permute-start.5
  47.3 0.2 slice.105
  47.5 0.5 slice.106
  48.0 4.3 %collective-permute-done.5 = f32[128,64]{1,0:T(8,128)S(1)} collective-permute-done((f32[128,64]{1,0:T(8,128)S(1)}, f32[128,64]{1,0:T(8,128)S(1)}, u32[]{:S(2)}, u32[]{:S(2)}) %collective-permute-start.5) | collective-permute-done | bytes 32800 | tf_op jit(solution)/shard_map/ppermute | solution.py:22
  52.3 0.1 slice_add_fusion
  52.4 1.9 %pad_maximum_fusion.2 = f32[128,8,448]{2,0,1:T(8,128)} fusion(f32[128,8,384]{2,0,1:T(8,128)S(1)} %slice.106, f32[128,8,64]{2,0,1:T(8,128)S(1)} %slice_add_fusion), kind=kLoop, calls=%fused_computation.6 | loop fusion | flops 458752 | bytes 3670016 | tf_op jit(solution)/shard_map/concatenate | solution.py:42
  54.3 2.8 %copy.25 = f32[128,8,448]{0,2,1:T(8,128)} copy(f32[128,8,448]{2,0,1:T(8,128)} %pad_maximum_fusion.2) | data formatting | bytes 3670016 | tf_op jit(solution)/shard_map/concatenate | solution.py:42
  57.2 2.8 %copy.26 = f32[128,3584]{1,0:T(8,128)} copy(f32[128,3584]{0,1:T(8,128)} %bitcast.40) | data formatting | bytes 3670016 | tf_op jit(solution)/shard_map/reshape | solution.py:43
  59.9 1.9 %fusion.6 = bf16[128,3584]{1,0:T(8,128)(2,1)S(1)} fusion(bf16[128,3584]{1,0:T(8,128)(2,1)S(1)} %fusion.2, f32[128,3584]{1,0:T(8,128)} %copy.26, bf16[128,3584]{1,0:T(8,128)(2,1)S(1)} %fusion.3), kind=kLoop, calls=%fused_computation.16 | loop fusion | flops 3211264 | bytes 4587520 | tf_op jit(solution)/shard_map/convert_element_type | solution.py:322
  61.9 12.9 %all_to_all.38 = bf16[128,4,896]{2,0,1:T(8,128)(2,1)} all-to-all(bf16[128,4,896]{2,0,1:T(8,128)(2,1)S(1)} %bitcast.41), channel_id=1, replica_groups=mesh['band'=4,'cell'=8] {'band'}, dimensions={1} | all-to-all | bytes 1835008 | tf_op jit(solution)/shard_map/all_to_all | solution.py:323
  74.8 25.6 %shard_map.46.packed_ref = f32[256,640]{1,0:T(8,128)} custom-call(bf16[512,896]{1,0:T(8,128)(2,1)} %bitcast.43), custom_call_target="tpu_custom_call" | custom-call | tf_op jit(solution)/shard_map/pallas_call | solution.py:176
  100.4 23.3 %shard_map.47 = bf16[512,512]{1,0:T(8,128)(2,1)} custom-call(f32[256,640]{1,0:T(8,128)} %shard_map.46.packed_ref), custom_call_target="tpu_custom_call" | custom-call | tf_op jit(solution)/shard_map/pallas_call | solution.py:290
  123.7 1.7 %convolution_convert_fusion = bf16[512,896]{1,0:T(8,128)(2,1)S(1)} fusion(bf16[512,512]{1,0:T(8,128)(2,1)} %shard_map.47, bf16[512,896]{1,0:T(8,128)(2,1)S(1)} %bitcast.44), kind=kOutput, calls=%fused_computation.17 | convolution fusion | flops 470220800 | bytes 2359296 | tf_op jit(solution)/shard_map/dot_general | solution.py:325
  125.5 16.0 %all_to_all.39 = bf16[4,128,896]{2,1,0:T(8,128)(2,1)S(1)} all-to-all(bf16[4,128,896]{2,1,0:T(8,128)(2,1)S(1)} %bitcast.49), channel_id=1, replica_groups=mesh['band'=4,'cell'=8] {'band'}, dimensions={0} | all-to-all | bytes 1835008 | tf_op jit(solution)/shard_map/all_to_all | solution.py:326
  141.4 1.0 copy.30
  (22 shorter events, 0.3 us)
Async XLA Ops:
  0.0 7.5 %copy-start = (bf16[512,512]{1,0:T(8,128)(2,1)S(1)}, bf16[512,512]{1,0:T(8,128)(2,1)}, u32[]{:S(2)}) copy-start(bf16[512,512]{1,0:T(8,128)(2,1)} %param.5) | copy-start | bytes 1572868
  0.8 6.7 %copy-start.3 = (f32[8,512]{1,0:T(8,128)S(1)}, f32[8,512]{1,0:T(8,128)}, u32[]{:S(2)}) copy-start(f32[8,512]{1,0:T(8,128)} %param.7) | copy-start | bytes 49156
  0.8 6.7 %copy-start.4 = (f32[8]{0:T(128)S(1)}, f32[8]{0:T(128)}, u32[]{:S(2)}) copy-start(f32[8]{0:T(128)} %param.6) | copy-start | bytes 100
  0.8 6.7 %collective-permute-start = (bf16[128,64]{1,0:T(8,128)(2,1)S(1)}, bf16[128,64]{1,0:T(8,128)(2,1)S(1)}, u32[]{:S(2)}, u32[]{:S(2)}) collective-permute-start(bf16[128,64]{1,0:T(8,128)(2,1)S(1)} %slice.73), channel_id=1, source_target_pairs={{1,0},{2,1},{3,2},{4,3},{5,4},{6,5},{7,6},{0,7},{9,8},{10,9},{11,1... | collective-permute-start | bytes 49160 | tf_op jit(solution)/shard_map/ppermute | solution.py:22
  8.4 5.5 %collective-permute-start.1 = (f32[128,64]{1,0:T(8,128)S(1)}, f32[128,64]{1,0:T(8,128)S(1)}, u32[]{:S(2)}, u32[]{:S(2)}) collective-permute-start(f32[128,64]{1,0:T(8,128)S(1)} %slice_bitcast_fusion.2), channel_id=1, source_target_pairs={{7,0},{0,1},{1,2},{2,3},{3,4},{4,5},{5,6},{6,7},{15,8},{8,9},{9,10... | collective-permute-start | bytes 98312 | tf_op jit(solution)/shard_map/ppermute | solution.py:22
  16.4 2.8 %copy-start.1 = (bf16[128,3584]{1,0:T(8,128)(2,1)S(1)}, bf16[128,3584]{1,0:T(8,128)(2,1)}, u32[]{:S(2)}) copy-start(bf16[128,3584]{1,0:T(8,128)(2,1)} %param.4) | copy-start | bytes 2752516
  21.0 3.0 %copy-start.5 = (f32[8]{0:T(128)S(1)}, f32[8]{0:T(128)}, u32[]{:S(2)}) copy-start(f32[8]{0:T(128)} %param.6) | copy-start | bytes 100
  21.0 2.9 %collective-permute-start.2 = (bf16[128,64]{1,0:T(8,128)(2,1)S(1)}, bf16[128,64]{1,0:T(8,128)(2,1)S(1)}, u32[]{:S(2)}, u32[]{:S(2)}) collective-permute-start(bf16[128,64]{1,0:T(8,128)(2,1)S(1)} %slice.96), channel_id=1, source_target_pairs={{1,0},{2,1},{3,2},{4,3},{5,4},{6,5},{7,6},{0,7},{9,8},{10,9},{11,1... | collective-permute-start | bytes 49160 | tf_op jit(solution)/shard_map/ppermute | solution.py:22
  26.4 5.5 %collective-permute-start.3 = (f32[128,64]{1,0:T(8,128)S(1)}, f32[128,64]{1,0:T(8,128)S(1)}, u32[]{:S(2)}, u32[]{:S(2)}) collective-permute-start(f32[128,64]{1,0:T(8,128)S(1)} %slice_bitcast_fusion.1), channel_id=1, source_target_pairs={{7,0},{0,1},{1,2},{2,3},{3,4},{4,5},{5,6},{6,7},{15,8},{8,9},{9,10... | collective-permute-start | bytes 98312 | tf_op jit(solution)/shard_map/ppermute | solution.py:22
  41.4 2.9 %collective-permute-start.4 = (bf16[128,64]{1,0:T(8,128)(2,1)S(1)}, bf16[128,64]{1,0:T(8,128)(2,1)S(1)}, u32[]{:S(2)}, u32[]{:S(2)}) collective-permute-start(bf16[128,64]{1,0:T(8,128)(2,1)S(1)} %slice.102), channel_id=1, source_target_pairs={{1,0},{2,1},{3,2},{4,3},{5,4},{6,5},{7,6},{0,7},{9,8},{10,9},{11,1... | collective-permute-start | bytes 49160 | tf_op jit(solution)/shard_map/ppermute | solution.py:22
  46.8 5.5 %collective-permute-start.5 = (f32[128,64]{1,0:T(8,128)S(1)}, f32[128,64]{1,0:T(8,128)S(1)}, u32[]{:S(2)}, u32[]{:S(2)}) collective-permute-start(f32[128,64]{1,0:T(8,128)S(1)} %slice_bitcast_fusion), channel_id=1, source_target_pairs={{7,0},{0,1},{1,2},{2,3},{3,4},{4,5},{5,6},{6,7},{15,8},{8,9},{9,10... | collective-permute-start | bytes 98312 | tf_op jit(solution)/shard_map/ppermute | solution.py:22
  74.8 48.9 %copy-start.2 = (bf16[128,4,896]{2,0,1:T(8,128)(2,1)S(1)}, bf16[128,4,896]{2,0,1:T(8,128)(2,1)}, u32[]{:S(2)}) copy-start(bf16[128,4,896]{2,0,1:T(8,128)(2,1)} %all_to_all.38) | copy-start | bytes 2752516
where the time goes:
time: 143 us; the launch traced here: 142 us
  Pallas kernels  48.9 us (34%)
  blocking collectives  28.8 us (20%)
  local copies, waits for them, and re-layouts  27.9 us (20%)
  waiting for transfers between devices  13.5 us (9%)
  other arithmetic  10.3 us (7%)
  matrix products  7.09 us (5%)
  starting transfers between devices  5.68 us (4%)
    pallas_call x1, Pallas kernels, margin_packed(): pl.pallas_call(functools.partial(reduce_kernel, count, bands, cells, tota...  25.6 us
    pallas_call x1, Pallas kernels, inverse_factor(): pl.pallas_call(functools.partial(factor_kernel, count), out_shape=jax.Sha...  23.3 us
    all_to_all x1, blocking collectives, shards(): lax.all_to_all(rotated, 'band', split_axis=0, concat_axis=1, tiled=True)  16 us
    ppermute x6, waiting for transfers between devices, shifted(): return lax.ppermute(block, axis, route)  13.5 us
    all_to_all x1, blocking collectives, shards(): lax.all_to_all(degree_three, 'band', split_axis=1, concat_axis=0, tiled=T...  12.9 us
    reshape x3, local copies, waits for them, and re-layouts, apply_h(): return kept.reshape(band_rows, cell_count * OWN)  8.38 us
    concatenate x3, local copies, waits for them, and re-layouts, apply_h(): kept = jnp.concatenate([kept[:, :, :PLANE] + spill, kept[:, :, PLANE:]], 2)  7.48 us
    ppermute x6, starting transfers between devices, shifted(): return lax.ppermute(block, axis, route)  5.68 us
  transfers between devices with their start and end apart: 6, of which 3 were waited for; matrix products, arithmetic and copies ran while one was open for 7% of the time, Pallas kernels for 0%

commit v1 on v0

--- a/solution.py
+++ b/solution.py
@@ -65,9 +65,42 @@
     packed_gram(slices_ref, packed_ref, count)
 
 
-def reduce_kernel(
-    count, bands, cells, total,
-    slices_ref, out_ref,
+def rows_at(start, size):
+    return pl.ds(pl.multiple_of(start, 8), size)
+
+
+def pair_step(e, degree, source, older, target, st, potb, potx):
+    at = lambda c, skip, size: pl.ds(pl.multiple_of(c * OWN + skip, 16), size)
+    nodes = OWN + PLANE
+    va, vb = source[at(e, 0, nodes), :], source[at(e + 1, 0, nodes), :]
+    vp = source[at(e - 1, 0, nodes), :]
+    both = jnp.dot(st[...], jnp.concatenate([va, vb], 1), preferred_element_type=jnp.float32)
+    before = jnp.dot(st[OWN:nodes, :], vp, preferred_element_type=jnp.float32)
+    scale = lambda c: potx[c][:, nodes:]
+    wa, wb = va.astype(jnp.float32), vb.astype(jnp.float32)
+    ya = scale(e) * both[:, :BLK] + potb[e] * wa
+    yb = scale(e + 1) * both[:, BLK:] + potb[e + 1] * wb
+    yp = scale(e - 1) * before + potb[e - 1, OWN:, :] * vp[OWN:].astype(jnp.float32)
+
+    def finish(c, h, w, skip):
+        size = h.shape[0]
+        value = h - centre * w
+        if degree == 1:
+            value = value * (1.0 / half_width)
+        else:
+            value = value * (2.0 / half_width) - older[at(c, skip, size), :].astype(jnp.float32)
+        target[at(c, skip, size), :] = value.astype(target.dtype)
+
+    finish(e, ya[:PLANE] + yp, wa[:PLANE], 0)
+    finish(e, ya[PLANE:OWN], wa[PLANE:OWN], PLANE)
+    finish(e + 1, yb[:PLANE] + ya[OWN:], wb[:PLANE], 0)
+    finish(e + 1, yb[PLANE:OWN], wb[PLANE:OWN], PLANE)
+
+
+def filter_kernel(
+    count, bands, cells, held, total,
+    wave_ref, stiff_ref, pots_ref, slices_ref, out_ref,
+    ext, one, two, three, st, potx, potb,
     mine, from_core, half, from_band, quarter, from_z, piece,
     send_sem, recv_sem,
 ):
@@ -79,22 +112,22 @@
     rows_half = mine.shape[0] // 2
     rows_band = rows_half // bands
     rows_z = rows_band // levels
+    nodes = OWN + PLANE
+    owned = held * OWN
 
     other_core = {"band": band, "cell": cell + 1 - 2 * core}
     band_peer = lambda o: lax.rem(band + o, bands)
     z_peer = lambda o: lax.rem(level + o, levels)
     band_device = lambda o: {"band": band_peer(o), "cell": cell}
     z_device = lambda o: {"band": band, "cell": z_peer(o) * 2 + core}
+    cell_device = lambda o: {"band": band, "cell": lax.rem(cell + o, cells)}
 
     barrier = pltpu.get_barrier_semaphore()
-    pl.semaphore_signal(barrier, inc=1, device_id=other_core, device_id_type=MESH)
     for o in range(1, bands):
         pl.semaphore_signal(barrier, inc=1, device_id=band_device(o), device_id_type=MESH)
-    for o in range(1, levels):
-        pl.semaphore_signal(barrier, inc=1, device_id=z_device(o), device_id_type=MESH)
-
-    packed_gram(slices_ref, mine, count)
-    pl.semaphore_wait(barrier, 1 + (bands - 1) + (levels - 1))
+    for o in range(1, cells):
+        pl.semaphore_signal(barrier, inc=1, device_id=cell_device(o), device_id_type=MESH)
+    pl.semaphore_wait(barrier, bands - 1 + cells - 1)
 
     used = [0]
 
@@ -108,31 +141,102 @@
         copy.start()
         return copy
 
-    def rows(start, size):
-        return pl.ds(pl.multiple_of(start, 8), size)
-
-    copy = send(mine.at[rows((1 - core) * rows_half, rows_half)], from_core, other_core)
+    low, high = 3 * OWN, 2 * OWN + PLANE
+    right, left = cell_device(1), cell_device(cells - 1)
+    halo = [
+        send(pots_ref.at[held - 3 : held], potx.at[0:3], right),
+        send(pots_ref.at[0:2], potx.at[held + 3 : held + 5], left),
+        send(wave_ref.at[owned - low : owned], ext.at[0:low], right),
+        send(wave_ref.at[0:high], ext.at[low + owned : low + owned + high], left),
+    ]
+    potx[3 : held + 3] = pots_ref[...]
+    ext[low : low + owned, :] = wave_ref[...]
+    st[...] = stiff_ref[...].T
+
+    def columns(c):
+        line = potx[c]
+        for q in range(nodes // BLK):
+            part = jnp.broadcast_to(line[:, q * BLK : (q + 1) * BLK], (BLK, BLK))
+            potb[c, q * BLK : (q + 1) * BLK, :] = part.T
+
+    @pl.loop(3, held + 3)
+    def _(c):
+        columns(c)
+
+    @pl.loop(0, (held - 4) // 2)
+    def _(p):
+        pair_step(5 + 2 * p, 1, ext, None, one, st, potb, potx)
+
+    for copy in halo:
+        copy.wait()
+    for c in (0, 1, 2, held + 3, held + 4):
+        columns(c)
+
+    @pl.loop(0, 4)
+    def _(p):
+        e = jnp.where(p < 2, 1 + 2 * p, held - 3 + 2 * p)
+        pair_step(e, 1, ext, None, one, st, potb, potx)
+
+    @pl.loop(0, held // 2 + 1)
+    def _(p):
+        pair_step(2 + 2 * p, 2, one, ext, two, st, potb, potx)
+
+    each = owned // bands
+    pairs = held // 2 // bands
+    base = used[0]
+    used[0] += bands - 1
+    swaps = []
+    for o in [*range(1, bands), 0]:
+        peer = band_peer(o)
+
+        @pl.loop(0, pairs)
+        def _(p):
+            pair_step(3 + 2 * (peer * pairs + p), 3, two, one, three, st, potb, potx)
+
+        piece_of = three.at[pl.ds(pl.multiple_of(low + peer * each, 16), each)]
+        if o:
+            copy = pltpu.make_async_remote_copy(
+                src_ref=piece_of, dst_ref=slices_ref.at[band],
+                send_sem=send_sem.at[base + o - 1], recv_sem=recv_sem.at[base + o - 1],
+                device_id=band_device(o), device_id_type=MESH,
+            )
+            copy.start()
+            swaps.append(copy)
+        else:
+            slices_ref[band] = piece_of[...]
+    for copy in swaps:
+        copy.wait()
+
+    for i in range(count):
+        row, col = place(i, 0, count)
+        width = (i + 1) * BLK
+        joined = jnp.concatenate([slices_ref[j] for j in range(i + 1)], 1)
+        mine[row : row + BLK, col : col + width] = jnp.dot(
+            slices_ref[i].T, joined, preferred_element_type=jnp.float32
+        )
+
+    copy = send(mine.at[rows_at((1 - core) * rows_half, rows_half)], from_core, other_core)
     copy.wait()
-    half[...] = mine[rows(core * rows_half, rows_half), :] + from_core[...]
+    half[...] = mine[rows_at(core * rows_half, rows_half), :] + from_core[...]
 
     copies = [
-        send(half.at[rows(band_peer(o) * rows_band, rows_band)], from_band.at[o - 1], band_device(o))
+        send(half.at[rows_at(band_peer(o) * rows_band, rows_band)], from_band.at[o - 1], band_device(o))
         for o in range(1, bands)
     ]
     for copy in copies:
         copy.wait()
-    summed = half[rows(band * rows_band, rows_band), :]
+    summed = half[rows_at(band * rows_band, rows_band), :]
     for o in range(1, bands):
         summed = summed + from_band[o - 1]
     quarter[...] = summed
 
     copies = [
-        send(quarter.at[rows(z_peer(o) * rows_z, rows_z)], from_z.at[o - 1], z_device(o))
+        send(quarter.at[rows_at(z_peer(o) * rows_z, rows_z)], from_z.at[o - 1], z_device(o))
         for o in range(1, levels)
     ]
     for copy in copies:
         copy.wait()
-    summed = quarter[rows(level * rows_z, rows_z), :]
+    summed = quarter[rows_at(level * rows_z, rows_z), :]
     for o in range(1, levels):
         summed = summed + from_z[o - 1]
     summed = summed / total
@@ -141,44 +245,54 @@
     start_half = core * rows_half
     start_band = start_half + band * rows_band
     start_z = start_band + level * rows_z
-    here = rows(start_z, rows_z)
+    here = rows_at(start_z, rows_z)
     out_ref[here, :] = summed
     copies = [send(piece, out_ref.at[here], z_device(o)) for o in range(1, levels)]
     for copy in copies:
         copy.wait()
-    here = out_ref.at[rows(start_band, rows_band)]
+    here = out_ref.at[rows_at(start_band, rows_band)]
     copies = [send(here, here, band_device(o)) for o in range(1, bands)]
     for copy in copies:
         copy.wait()
-    here = out_ref.at[rows(start_half, rows_half)]
+    here = out_ref.at[rows_at(start_half, rows_half)]
     send(here, here, other_core).wait()
 
 
-def margin_packed(slices):
+def filtered(wavefunctions, stiffness, cell_scale, potential):
     bands, cells = lax.axis_size("band"), lax.axis_size("cell")
-    band_total, nodes = slices.shape
-    count = band_total // BLK
-    total = float(nodes * bands * cells)
-    height, width = band_total // 2, (count + 1) * BLK
-    shape = jax.ShapeDtypeStruct((height, width), jnp.float32)
-    vmem = pl.BlockSpec(memory_space=pltpu.VMEM)
-    if cells % 2 or cells < 4 or bands < 2 or height % (8 * bands * cells):
-        partial = pl.pallas_call(
-            functools.partial(gram_kernel, count), out_shape=shape, in_specs=[vmem], out_specs=vmem
-        )(slices)
-        return lax.psum(partial, ("band", "cell")) / total
+    band_rows, owned = wavefunctions.shape
+    held = owned // OWN
+    nodes = OWN + PLANE
+    count = band_rows * bands // BLK
+    each = owned // bands
+    total = float(owned * cells)
+    height, width = count * BLK // 2, (count + 1) * BLK
     levels = cells // 2
     rows_half = height // 2
     rows_band = rows_half // bands
     rows_z = rows_band // levels
-    sends = 2 * (1 + (bands - 1) + (levels - 1))
-    f32 = jnp.float32
+    sends = 4 + (bands - 1) + 2 * (1 + (bands - 1) + (levels - 1))
+    spans = owned + 5 * OWN + PLANE
+    scales = jnp.broadcast_to(cell_scale[:, None], (held, BLK))
+    pots = jnp.concatenate([potential, scales], 1)[:, None, :]
+    vmem = pl.BlockSpec(memory_space=pltpu.VMEM)
+    f32, bf16 = jnp.float32, jnp.bfloat16
     return pl.pallas_call(
-        functools.partial(reduce_kernel, count, bands, cells, total),
-        out_shape=shape,
-        in_specs=[vmem],
-        out_specs=vmem,
+        functools.partial(filter_kernel, count, bands, cells, held, total),
+        out_shape=(
+            jax.ShapeDtypeStruct((bands, each, BLK), bf16),
+            jax.ShapeDtypeStruct((height, width), f32),
+        ),
+        in_specs=[vmem] * 3,
+        out_specs=(vmem, vmem),
         scratch_shapes=[
+            pltpu.VMEM((spans, BLK), bf16),
+            pltpu.VMEM((spans, BLK), bf16),
+            pltpu.VMEM((spans, BLK), bf16),
+            pltpu.VMEM((spans, BLK), bf16),
+            pltpu.VMEM((nodes, nodes), bf16),
+            pltpu.VMEM((held + 5, 1, nodes + BLK), f32),
+            pltpu.VMEM((held + 5, nodes, BLK), f32),
             pltpu.VMEM((height, width), f32),
             pltpu.VMEM((rows_half, width), f32),
             pltpu.VMEM((rows_half, width), f32),
@@ -190,7 +304,83 @@
             pltpu.SemaphoreType.DMA((sends,)),
         ],
         compiler_params=pltpu.CompilerParams(collective_id=0, has_side_effects=True),
+    )(wavefunctions.T, stiffness, pots)
+
+
+def rotate_kernel(bands, inverse_ref, slices_ref, out_ref, rotated, send_sem, recv_sem):
+    band = lax.axis_index("band")
+    cell = lax.axis_index("cell")
+    each = slices_ref.shape[1]
+    peer = lambda o: lax.rem(band + o, bands)
+    device = lambda o: {"band": peer(o), "cell": cell}
+    barrier = pltpu.get_barrier_semaphore()
+    for o in range(1, bands):
+        pl.semaphore_signal(barrier, inc=1, device_id=device(o), device_id_type=MESH)
+    pl.semaphore_wait(barrier, bands - 1)
+    joined = jnp.concatenate([slices_ref[j] for j in range(bands)], 1)
+    here = pl.ds(pl.multiple_of(band * each, BLK), each)
+    copies = []
+    for o in [*range(1, bands), 0]:
+        some = inverse_ref[rows_at(peer(o) * BLK, BLK), :]
+        value = lax.dot_general(
+            some, joined, (((1,), (1,)), ((), ())), preferred_element_type=jnp.float32
+        ).astype(out_ref.dtype)
+        if o == 0:
+            out_ref[:, here] = value
+            continue
+        rotated[o - 1] = value
+        copy = pltpu.make_async_remote_copy(
+            src_ref=rotated.at[o - 1], dst_ref=out_ref.at[:, here],
+            send_sem=send_sem.at[o - 1], recv_sem=recv_sem.at[o - 1],
+            device_id=device(o), device_id_type=MESH,
+        )
+        copy.start()
+        copies.append(copy)
+    for copy in copies:
+        copy.wait()
+
+
+def rotated_back(inverse, slices):
+    bands, each, wide = slices.shape
+    vmem = pl.BlockSpec(memory_space=pltpu.VMEM)
+    return pl.pallas_call(
+        functools.partial(rotate_kernel, bands),
+        out_shape=jax.ShapeDtypeStruct((wide, bands * each), slices.dtype),
+        in_specs=[vmem, vmem],
+        out_specs=vmem,
+        scratch_shapes=[
+            pltpu.VMEM((bands - 1, wide, each), slices.dtype),
+            pltpu.SemaphoreType.DMA((bands - 1,)),
+            pltpu.SemaphoreType.DMA((bands - 1,)),
+        ],
+        compiler_params=pltpu.CompilerParams(collective_id=1, has_side_effects=True),
+    )(inverse, slices)
+
+
+def fits(band_rows, owned, bands, cells):
+    height = band_rows * bands // 2
+    return (
+        band_rows == BLK
+        and owned % OWN == 0
+        and bands >= 2
+        and cells % 2 == 0
+        and cells >= 4
+        and owned // OWN >= 4
+        and owned // OWN % (2 * bands) == 0
+        and height % (16 * bands * (cells // 2)) == 0
+    )
+
+
+def margin_packed(slices):
+    bands, cells = lax.axis_size("band"), lax.axis_size("cell")
+    band_total, nodes = slices.shape
+    count = band_total // BLK
+    shape = jax.ShapeDtypeStruct((band_total // 2, (count + 1) * BLK), jnp.float32)
+    vmem = pl.BlockSpec(memory_space=pltpu.VMEM)
+    partial = pl.pallas_call(
+        functools.partial(gram_kernel, count), out_shape=shape, in_specs=[vmem], out_specs=vmem
     )(slices)
+    return lax.psum(partial, ("band", "cell")) / float(nodes * bands * cells)
 
 
 def invert_block(block_ref):
@@ -302,6 +492,9 @@
 
 
 def shards(wavefunctions, stiffness, cell_scale, potential):
+    if fits(*wavefunctions.shape, lax.axis_size("band"), lax.axis_size("cell")):
+        slices, packed = filtered(wavefunctions, stiffness, cell_scale, potential)
+        return rotated_back(inverse_factor(packed), slices)
     anchor = wavefunctions.astype(jnp.float32)
     degree_one = (
         (apply_h(wavefunctions, stiffness, cell_scale, potential) - centre * anchor) / half_width

time: 143 us -> 101 us (0.71)
  Pallas kernels: 48.9 us -> 93.9 us
  blocking collectives: 28.8 us -> 0 us
  local copies, waits for them, and re-layouts: 27.9 us -> 5.71 us
  waiting for transfers between devices: 13.5 us -> 0 us
  other arithmetic: 10.3 us -> 0.72 us
  matrix products: 7.09 us -> 0 us
  starting transfers between devices: 5.68 us -> 0 us
    pallas_call x1 -> x2, Pallas kernels: 25.6 us -> 70.6 us  [the longest x1 54.1 us: filtered(): pl.pallas_call(functools.partial(filter_kernel, count, bands, cells, held...]
    all_to_all x2 -> x0, blocking collectives: 28.8 us -> none  [the longest x1 16 us: shards(): lax.all_to_all(rotated, 'band', split_axis=0, concat_axis=1, tiled=True)]
    ppermute x6 -> x0, waiting for transfers between devices: 13.5 us -> none  [shifted(): return lax.ppermute(block, axis, route)]
    reshape x6 -> x0, local copies, waits for them, and re-layouts: 11.5 us -> none  [the longest x3 8.38 us: apply_h(): return kept.reshape(band_rows, cell_count * OWN)]
    concatenate x3 -> x0, local copies, waits for them, and re-layouts: 7.48 us -> none  [apply_h(): kept = jnp.concatenate([kept[:, :, :PLANE] + spill, kept[:, :, PLANE:]], 2)]
    dot_general x4 -> x0, matrix products: 7.09 us -> none  [the longest x3 5.34 us: apply_h(): jnp.einsum('bcn,nm->bcm', cell_nodes, stiffness, preferred_element_type=j...]
    ppermute x6 -> x0, starting transfers between devices: 5.68 us -> none  [shifted(): return lax.ppermute(block, axis, route)]
    convert_element_type x3 -> x0, other arithmetic: 5.54 us -> none  [the longest x1 1.89 us: shards(): degree_three = (2.0 * (apply_h(degree_two, stiffness, cell_scale, potenti...]
  transfers between devices with their start and end apart: 6 -> 0, of which waited for: 3 -> 0; matrix products, arithmetic and copies ran while one was open for 7% -> 0% of each run, Pallas kernels for 0% -> 0%
where the time goes in v1:
time: 101 us; the launch traced here: 100 us
  Pallas kernels  93.9 us (93%)
  local copies, waits for them, and re-layouts  5.71 us (6%)
    pallas_call x1, Pallas kernels, filtered(): pl.pallas_call(functools.partial(filter_kernel, count, bands, cells, held...  54.1 us
    pallas_call x1, Pallas kernels, inverse_factor(): pl.pallas_call(functools.partial(factor_kernel, count), out_shape=jax.Sha...  23.3 us
    pallas_call x1, Pallas kernels, rotated_back(): pl.pallas_call(functools.partial(rotate_kernel, bands), out_shape=jax.Sha...  16.5 us
    unnamed x2, local copies, waits for them, and re-layouts  4.37 us

profile of v1, /device:TPU:0, one launch (start us, length us, event | category | flops | bytes accessed | tf_op | source)
XLA Modules:
  0.0 100.4 jit_solution(2872052195822403059)
XLA Ops:
  0.0 0.7 broadcast_in_dim.4
  0.7 0.7 pad_maximum_fusion
  1.4 0.6 broadcast_in_dim.10.pots_ref
  2.1 2.2 %copy.5 = bf16[128,3584]{0,1:T(8,128)(2,1)} copy(bf16[128,3584]{1,0:T(8,128)(2,1)} %param.4) | data formatting | bytes 1835008 | tf_op args[0]
  4.3 54.1 %shard_map.46 = (bf16[4,896,128]{2,1,0:T(8,128)(2,1)}, f32[256,640]{1,0:T(8,128)}) custom-call(bf16[3584,128]{1,0:T(8,128)(2,1)} %bitcast.1, bf16[512,512]{1,0:T(8,128)(2,1)} %stiff_ref.1, f32[8,1,640]{2,1,0:T(1,128)} %broadcast_in_dim.10.pots_ref), custom_call_target="tpu_custom_call" | custom-call | tf_op jit(solution)/shard_map/pallas_call | solution.py:280
  58.4 23.3 %shard_map.47.inverse_ref = bf16[512,512]{1,0:T(8,128)(2,1)} custom-call(f32[256,640]{1,0:T(8,128)} %get-tuple-element.7.packed_ref), custom_call_target="tpu_custom_call" | custom-call | tf_op jit(solution)/shard_map/pallas_call | solution.py:480
  81.7 16.5 %shard_map.48 = bf16[128,3584]{1,0:T(8,128)(2,1)} custom-call(bf16[512,512]{1,0:T(8,128)(2,1)} %shard_map.47.inverse_ref, bf16[4,896,128]{2,1,0:T(8,128)(2,1)} %get-tuple-element.8.slices_ref), custom_call_target="tpu_custom_call" | custom-call | tf_op jit(solution)/shard_map/pallas_call | solution.py:346
  98.2 2.2 %copy.7 = bf16[128,3584]{1,0:T(8,128)(2,1)} copy(bf16[128,3584]{1,0:T(8,128)(2,1)} %shard_map.48) | data formatting | bytes 1835008

commit v2 on v1

--- a/solution.py
+++ b/solution.py
@@ -99,8 +99,8 @@
 
 def filter_kernel(
     count, bands, cells, held, total,
-    wave_ref, stiff_ref, pots_ref, slices_ref, out_ref,
-    ext, one, two, three, st, potx, potb,
+    wave_ref, stiff_ref, scale_ref, potential_ref, slices_ref, out_ref,
+    pots, turned, ext, one, two, three, st, potx, potb,
     mine, from_core, half, from_band, quarter, from_z, piece,
     send_sem, recv_sem,
 ):
@@ -127,8 +127,6 @@
         pl.semaphore_signal(barrier, inc=1, device_id=band_device(o), device_id_type=MESH)
     for o in range(1, cells):
         pl.semaphore_signal(barrier, inc=1, device_id=cell_device(o), device_id_type=MESH)
-    pl.semaphore_wait(barrier, bands - 1 + cells - 1)
-
     used = [0]
 
     def send(src, dst, device):
@@ -143,14 +141,31 @@
 
     low, high = 3 * OWN, 2 * OWN + PLANE
     right, left = cell_device(1), cell_device(cells - 1)
+
+    def turn(q):
+        span = slice(q * BLK, (q + 1) * BLK)
+        turned[span, :] = wave_ref[:, span].T
+
+    strips = owned // BLK
+    first, last = -(-high // BLK), (owned - low) // BLK
+    for c in range(held):
+        pots[c, :, :nodes] = potential_ref[c : c + 1, :]
+        pots[c, :, nodes:] = jnp.broadcast_to(scale_ref[:, c : c + 1], (1, BLK))
+    for q in range(last, strips):
+        turn(q)
+    pl.semaphore_wait(barrier, bands - 1 + cells - 1)
     halo = [
-        send(pots_ref.at[held - 3 : held], potx.at[0:3], right),
-        send(pots_ref.at[0:2], potx.at[held + 3 : held + 5], left),
-        send(wave_ref.at[owned - low : owned], ext.at[0:low], right),
-        send(wave_ref.at[0:high], ext.at[low + owned : low + owned + high], left),
+        send(pots.at[held - 3 : held], potx.at[0:3], right),
+        send(pots.at[0:2], potx.at[held + 3 : held + 5], left),
+        send(turned.at[owned - low : owned], ext.at[0:low], right),
     ]
-    potx[3 : held + 3] = pots_ref[...]
-    ext[low : low + owned, :] = wave_ref[...]
+    for q in range(first):
+        turn(q)
+    halo.append(send(turned.at[0:high], ext.at[low + owned : low + owned + high], left))
+    for q in range(first, last):
+        turn(q)
+    potx[3 : held + 3] = pots[...]
+    ext[low : low + owned, :] = turned[...]
     st[...] = stiff_ref[...].T
 
     def columns(c):
@@ -273,8 +288,6 @@
     rows_z = rows_band // levels
     sends = 4 + (bands - 1) + 2 * (1 + (bands - 1) + (levels - 1))
     spans = owned + 5 * OWN + PLANE
-    scales = jnp.broadcast_to(cell_scale[:, None], (held, BLK))
-    pots = jnp.concatenate([potential, scales], 1)[:, None, :]
     vmem = pl.BlockSpec(memory_space=pltpu.VMEM)
     f32, bf16 = jnp.float32, jnp.bfloat16
     return pl.pallas_call(
@@ -283,9 +296,11 @@
             jax.ShapeDtypeStruct((bands, each, BLK), bf16),
             jax.ShapeDtypeStruct((height, width), f32),
         ),
-        in_specs=[vmem] * 3,
+        in_specs=[vmem] * 4,
         out_specs=(vmem, vmem),
         scratch_shapes=[
+            pltpu.VMEM((held, 1, nodes + BLK), f32),
+            pltpu.VMEM((owned, BLK), bf16),
             pltpu.VMEM((spans, BLK), bf16),
             pltpu.VMEM((spans, BLK), bf16),
             pltpu.VMEM((spans, BLK), bf16),
@@ -304,7 +319,7 @@
             pltpu.SemaphoreType.DMA((sends,)),
         ],
         compiler_params=pltpu.CompilerParams(collective_id=0, has_side_effects=True),
-    )(wavefunctions.T, stiffness, pots)
+    )(wavefunctions, stiffness, cell_scale[None, :], potential)
 
 
 def rotate_kernel(bands, inverse_ref, slices_ref, out_ref, rotated, send_sem, recv_sem):

time: 101 us -> 96.5 us (0.955)
  local copies, waits for them, and re-layouts: 5.71 us -> 2.16 us
    unnamed x2 -> x1, local copies, waits for them, and re-layouts: 4.37 us -> 2.16 us
    broadcast_in_dim x2 -> x0, local copies, waits for them, and re-layouts: 1.35 us -> none  [the longest x1 0.72 us: filtered(): scales = jnp.broadcast_to(cell_scale[:, None], (held, BLK))]
where the time goes in v2:
time: 96.5 us; the launch traced here: 96.3 us
  Pallas kernels  94.1 us (98%)
  local copies, waits for them, and re-layouts  2.16 us (2%)
    pallas_call x1, Pallas kernels, filtered(): pl.pallas_call(functools.partial(filter_kernel, count, bands, cells, held...  54.3 us
    pallas_call x1, Pallas kernels, inverse_factor(): pl.pallas_call(functools.partial(factor_kernel, count), out_shape=jax.Sha...  23.3 us
    pallas_call x1, Pallas kernels, rotated_back(): pl.pallas_call(functools.partial(rotate_kernel, bands), out_shape=jax.Sha...  16.5 us
    unnamed x1, local copies, waits for them, and re-layouts  2.16 us

profile of v2, /device:TPU:0, one launch (start us, length us, event | category | flops | bytes accessed | tf_op | source)
XLA Modules:
  0.0 96.3 jit_solution(6377960354207941840)
XLA Ops:
  0.0 54.3 %shard_map.46 = (bf16[4,896,128]{2,1,0:T(8,128)(2,1)}, f32[256,640]{1,0:T(8,128)}) custom-call(bf16[128,3584]{1,0:T(8,128)(2,1)} %wave_ref.1, bf16[512,512]{1,0:T(8,128)(2,1)} %stiff_ref.1, f32[1,8]{1,0:T(1,128)} %bitcast.1, f32[8,512]{1,0:T(8,128)} %potential_ref.1), custom_call_target="tpu_custom_call" | custom-call | tf_op jit(solution)/shard_map/pallas_call | solution.py:293
  54.3 23.3 %shard_map.47.inverse_ref = bf16[512,512]{1,0:T(8,128)(2,1)} custom-call(f32[256,640]{1,0:T(8,128)} %get-tuple-element.7.packed_ref), custom_call_target="tpu_custom_call" | custom-call | tf_op jit(solution)/shard_map/pallas_call | solution.py:495
  77.6 16.5 %shard_map.48 = bf16[128,3584]{1,0:T(8,128)(2,1)} custom-call(bf16[512,512]{1,0:T(8,128)(2,1)} %shard_map.47.inverse_ref, bf16[4,896,128]{2,1,0:T(8,128)(2,1)} %get-tuple-element.8.slices_ref), custom_call_target="tpu_custom_call" | custom-call | tf_op jit(solution)/shard_map/pallas_call | solution.py:361
  94.1 2.2 %copy.6 = bf16[128,3584]{1,0:T(8,128)(2,1)} copy(bf16[128,3584]{1,0:T(8,128)(2,1)} %shard_map.48) | data formatting | bytes 1835008

commit v3 on v2

--- a/solution.py
+++ b/solution.py
@@ -69,7 +69,7 @@
     return pl.ds(pl.multiple_of(start, 8), size)
 
 
-def pair_step(e, degree, source, older, target, st, potb, potx):
+def pair_step(e, degree, source, older, target, st, potb, potx, shift=0):
     at = lambda c, skip, size: pl.ds(pl.multiple_of(c * OWN + skip, 16), size)
     nodes = OWN + PLANE
     va, vb = source[at(e, 0, nodes), :], source[at(e + 1, 0, nodes), :]
@@ -89,7 +89,7 @@
             value = value * (1.0 / half_width)
         else:
             value = value * (2.0 / half_width) - older[at(c, skip, size), :].astype(jnp.float32)
-        target[at(c, skip, size), :] = value.astype(target.dtype)
+        target[at(c - shift, skip, size), :] = value.astype(target.dtype)
 
     finish(e, ya[:PLANE] + yp, wa[:PLANE], 0)
     finish(e, ya[PLANE:OWN], wa[PLANE:OWN], PLANE)
@@ -97,10 +97,52 @@
     finish(e + 1, yb[PLANE:OWN], wb[PLANE:OWN], PLANE)
 
 
+def send_ahead(turns, bands, band, cell, own_ref, ahead_ref, send_sem, recv_sem, base):
+    each = ahead_ref.shape[2]
+    wide = len(turns)
+    device = lambda b: {"band": b, "cell": cell}
+
+    def copy_to(b, n):
+        part = (b + 1 + turns[n]) % bands
+        return pltpu.make_async_remote_copy(
+            src_ref=own_ref.at[part * each : (part + 1) * each], dst_ref=ahead_ref.at[band, n],
+            send_sem=send_sem.at[base + (b - 1) * wide + n], recv_sem=recv_sem.at[base + band * wide + n],
+            device_id=device(b), device_id_type=MESH,
+        )
+
+    def copy_from(h, n):
+        return pltpu.make_async_remote_copy(
+            src_ref=own_ref.at[0:each], dst_ref=ahead_ref.at[h, n],
+            send_sem=send_sem.at[base + n], recv_sem=recv_sem.at[base + h * wide + n],
+            device_id=device(h), device_id_type=MESH,
+        )
+
+    for n in range(wide):
+        for b in range(1, bands):
+
+            @pl.when(band < b)
+            def _():
+                copy_to(b, n).start()
+
+    def finish():
+        for n in range(wide):
+            for b in range(1, bands):
+
+                @pl.when(band < b)
+                def _():
+                    copy_to(b, n).wait_send()
+
+                @pl.when(b - 1 < band)
+                def _():
+                    copy_from(b - 1, n).wait_recv()
+
+    return finish
+
+
 def filter_kernel(
     count, bands, cells, held, total,
-    wave_ref, stiff_ref, scale_ref, potential_ref, slices_ref, out_ref,
-    pots, turned, ext, one, two, three, st, potx, potb,
+    wave_ref, stiff_ref, scale_ref, potential_ref, slices_ref, three, ahead_ref, out_ref,
+    pots, turned, ext, one, two, st, potx, potb,
     mine, from_core, half, from_band, quarter, from_z, piece,
     send_sem, recv_sem,
 ):
@@ -206,9 +248,9 @@
 
         @pl.loop(0, pairs)
         def _(p):
-            pair_step(3 + 2 * (peer * pairs + p), 3, two, one, three, st, potb, potx)
-
-        piece_of = three.at[pl.ds(pl.multiple_of(low + peer * each, 16), each)]
+            pair_step(3 + 2 * (peer * pairs + p), 3, two, one, three, st, potb, potx, 3)
+
+        piece_of = three.at[pl.ds(pl.multiple_of(peer * each, 16), each)]
         if o:
             copy = pltpu.make_async_remote_copy(
                 src_ref=piece_of, dst_ref=slices_ref.at[band],
@@ -249,6 +291,9 @@
         send(quarter.at[rows_at(z_peer(o) * rows_z, rows_z)], from_z.at[o - 1], z_device(o))
         for o in range(1, levels)
     ]
+    finish_ahead = send_ahead(
+        range(0, 1), bands, band, cell, three, ahead_ref, send_sem, recv_sem, send_sem.shape[0] - bands + 1
+    )
     for copy in copies:
         copy.wait()
     summed = quarter[rows_at(level * rows_z, rows_z), :]
@@ -271,6 +316,7 @@
         copy.wait()
     here = out_ref.at[rows_at(start_half, rows_half)]
     send(here, here, other_core).wait()
+    finish_ahead()
 
 
 def filtered(wavefunctions, stiffness, cell_scale, potential):
@@ -286,7 +332,7 @@
     rows_half = height // 2
     rows_band = rows_half // bands
     rows_z = rows_band // levels
-    sends = 4 + (bands - 1) + 2 * (1 + (bands - 1) + (levels - 1))
+    sends = 4 + 2 * (bands - 1) + 2 * (1 + (bands - 1) + (levels - 1))
     spans = owned + 5 * OWN + PLANE
     vmem = pl.BlockSpec(memory_space=pltpu.VMEM)
     f32, bf16 = jnp.float32, jnp.bfloat16
@@ -294,14 +340,15 @@
         functools.partial(filter_kernel, count, bands, cells, held, total),
         out_shape=(
             jax.ShapeDtypeStruct((bands, each, BLK), bf16),
+            jax.ShapeDtypeStruct((owned, BLK), bf16),
+            jax.ShapeDtypeStruct((bands - 1, 1, each, BLK), bf16),
             jax.ShapeDtypeStruct((height, width), f32),
         ),
         in_specs=[vmem] * 4,
-        out_specs=(vmem, vmem),
+        out_specs=(vmem,) * 4,
         scratch_shapes=[
             pltpu.VMEM((held, 1, nodes + BLK), f32),
             pltpu.VMEM((owned, BLK), bf16),
-            pltpu.VMEM((spans, BLK), bf16),
             pltpu.VMEM((spans, BLK), bf16),
             pltpu.VMEM((spans, BLK), bf16),
             pltpu.VMEM((spans, BLK), bf16),
@@ -322,54 +369,35 @@
     )(wavefunctions, stiffness, cell_scale[None, :], potential)
 
 
-def rotate_kernel(bands, inverse_ref, slices_ref, out_ref, rotated, send_sem, recv_sem):
+def rotate_kernel(bands, inverse_ref, slices_ref, own_ref, first_ref, rest_ref, out_ref):
     band = lax.axis_index("band")
-    cell = lax.axis_index("cell")
     each = slices_ref.shape[1]
-    peer = lambda o: lax.rem(band + o, bands)
-    device = lambda o: {"band": peer(o), "cell": cell}
-    barrier = pltpu.get_barrier_semaphore()
-    for o in range(1, bands):
-        pl.semaphore_signal(barrier, inc=1, device_id=device(o), device_id_type=MESH)
-    pl.semaphore_wait(barrier, bands - 1)
-    joined = jnp.concatenate([slices_ref[j] for j in range(bands)], 1)
-    here = pl.ds(pl.multiple_of(band * each, BLK), each)
-    copies = []
-    for o in [*range(1, bands), 0]:
-        some = inverse_ref[rows_at(peer(o) * BLK, BLK), :]
-        value = lax.dot_general(
-            some, joined, (((1,), (1,)), ((), ())), preferred_element_type=jnp.float32
-        ).astype(out_ref.dtype)
-        if o == 0:
-            out_ref[:, here] = value
-            continue
-        rotated[o - 1] = value
-        copy = pltpu.make_async_remote_copy(
-            src_ref=rotated.at[o - 1], dst_ref=out_ref.at[:, here],
-            send_sem=send_sem.at[o - 1], recv_sem=recv_sem.at[o - 1],
-            device_id=device(o), device_id_type=MESH,
-        )
-        copy.start()
-        copies.append(copy)
-    for copy in copies:
-        copy.wait()
-
-
-def rotated_back(inverse, slices):
-    bands, each, wide = slices.shape
+    for g in range(bands):
+
+        @pl.when(band == g)
+        def _():
+            some = inverse_ref[g * BLK : (g + 1) * BLK, : (g + 1) * BLK]
+            for r in range(bands):
+                part = (g + r) % bands
+                here = slice(part * each, (part + 1) * each)
+                lower = lambda h: (
+                    slices_ref[h] if r == 0 else first_ref[h, 0] if r == 1 else rest_ref[h, r - 2]
+                )
+                joined = jnp.concatenate([lower(h) for h in range(g)] + [own_ref[here, :]], 1)
+                out_ref[:, here] = lax.dot_general(
+                    some, joined, (((1,), (1,)), ((), ())), preferred_element_type=jnp.float32
+                ).astype(out_ref.dtype)
+
+
+def rotated_here(inverse, slices, own, first, rest):
+    bands = slices.shape[0]
     vmem = pl.BlockSpec(memory_space=pltpu.VMEM)
     return pl.pallas_call(
         functools.partial(rotate_kernel, bands),
-        out_shape=jax.ShapeDtypeStruct((wide, bands * each), slices.dtype),
-        in_specs=[vmem, vmem],
+        out_shape=jax.ShapeDtypeStruct(own.shape[::-1], own.dtype),
+        in_specs=[vmem] * 5,
         out_specs=vmem,
-        scratch_shapes=[
-            pltpu.VMEM((bands - 1, wide, each), slices.dtype),
-            pltpu.SemaphoreType.DMA((bands - 1,)),
-            pltpu.SemaphoreType.DMA((bands - 1,)),
-        ],
-        compiler_params=pltpu.CompilerParams(collective_id=1, has_side_effects=True),
-    )(inverse, slices)
+    )(inverse, slices, own, first, rest)
 
 
 def fits(band_rows, owned, bands, cells):
@@ -377,7 +405,7 @@
     return (
         band_rows == BLK
         and owned % OWN == 0
-        and bands >= 2
+        and bands >= 3
         and cells % 2 == 0
         and cells >= 4
         and owned // OWN >= 4
@@ -401,47 +429,55 @@
 def invert_block(block_ref):
     tiles = BLK // PAN
     shape = (PAN, BLK)
-    lane = lax.broadcasted_iota(jnp.int32, shape, 1)
+    lane = lax.broadcasted_iota(jnp.int32, (tiles, *shape), 2)
+    line = lax.broadcasted_iota(jnp.int32, (tiles, *shape), 1)
+    tile = lax.broadcasted_iota(jnp.int32, (tiles, *shape), 0)
     row = lax.broadcasted_iota(jnp.int32, shape, 0)
-    left = [block_ref[t * PAN : (t + 1) * PAN, :] for t in range(tiles)]
-    right = [jnp.where(lane == row + t * PAN, 1.0, 0.0).astype(jnp.float32) for t in range(tiles)]
+    left = block_ref[...].reshape(tiles, *shape)
+    right = jnp.where(lane == line + tile * PAN, 1.0, 0.0).astype(jnp.float32)
 
     def spread(value):
-        return jnp.broadcast_to(value, shape)
+        return jnp.broadcast_to(value, (1, *shape))
 
     for m in range(tiles):
         k = m * PAN
-        grid = {
-            (i, j): spread(left[m][i : i + 1, k + j : k + j + 1])
+        now_left, now_right = left[0], right[0]
+        more = m + 1 < tiles
+        grid = [
+            jnp.concatenate(
+                [spread(now_left[i : i + 1, k + j : k + j + 1][None]) for i in range(j, PAN)], 0
+            )
             for j in range(PAN)
-            for i in range(j, PAN)
-        }
-        cols = [
-            [spread(left[t][:, k + j : k + j + 1]) for t in range(m + 1, tiles)] for j in range(PAN)
         ]
-        rows_left = [spread(left[m][j : j + 1, :]) for j in range(PAN)]
-        rows_right = [spread(right[m][j : j + 1, :]) for j in range(PAN)]
+        rows_left = jnp.concatenate([spread(now_left[j : j + 1, :][None]) for j in range(PAN)], 0)
+        rows_right = jnp.concatenate([spread(now_right[j : j + 1, :][None]) for j in range(PAN)], 0)
+        if more:
+            left, right = left[1:], right[1:]
+            cols = jnp.concatenate(
+                [
+                    jnp.broadcast_to(left[:, :, k + j : k + j + 1], left.shape)[None]
+                    for j in range(PAN)
+                ],
+                0,
+            )
+        done = None
         for j in range(PAN):
-            scale = lax.rsqrt(grid[j, j])
-            rows_left[j] = rows_left[j] * scale
-            rows_right[j] = rows_right[j] * scale
-            cols[j] = [c * scale for c in cols[j]]
-            factor = {i: grid[i, j] * scale for i in range(j + 1, PAN)}
-            for i in range(j + 1, PAN):
-                for q in range(j + 1, i + 1):
-                    grid[i, q] = grid[i, q] - factor[i] * factor[q]
-                rows_left[i] = rows_left[i] - factor[i] * rows_left[j]
-                rows_right[i] = rows_right[i] - factor[i] * rows_right[j]
-                cols[i] = [c - factor[i] * d for c, d in zip(cols[i], cols[j])]
-        for n, t in enumerate(range(m + 1, tiles)):
-            for j in range(PAN):
-                left[t] = left[t] - cols[j][n] * rows_left[j]
-                right[t] = right[t] - cols[j][n] * rows_right[j]
-        done = rows_right[0]
-        for j in range(1, PAN):
-            done = jnp.where(row == j, rows_right[j], done)
-        right[m] = done
-    return right
+            scale = lax.rsqrt(grid[j][0])
+            head_left, head_right = rows_left[0] * scale, rows_right[0] * scale
+            done = head_right if j == 0 else jnp.where(row == j, head_right, done)
+            if j + 1 < PAN:
+                factor = grid[j][1:] * scale
+                for q in range(j + 1, PAN):
+                    grid[q] = grid[q] - factor[q - j - 1 :] * factor[q - j - 1]
+                rows_left = rows_left[1:] - factor * head_left
+                rows_right = rows_right[1:] - factor * head_right
+            if more:
+                head = cols[0] * scale
+                left = left - head * head_left
+                right = right - head * head_right
+                if j + 1 < PAN:
+                    cols = cols[1:] - factor[:, None] * head[None]
+        block_ref[k : k + PAN, :] = done
 
 
 def exact(a, b, dims):
@@ -454,7 +490,24 @@
 NT = ((1,), (1,))
 
 
-def factor_kernel(count, packed_ref, out_ref, work, lower, inv, diag):
+def factor_kernel(
+    count, bands, packed_ref, own_ref, out_ref, rest_ref, work, lower, inv, diag, send_sem, recv_sem
+):
+    band = lax.axis_index("band")
+    cell = lax.axis_index("cell")
+    barrier = pltpu.get_barrier_semaphore()
+    for o in range(1, bands):
+        device = {"band": lax.rem(band + o, bands), "cell": cell}
+        pl.semaphore_signal(barrier, inc=1, device_id=device, device_id_type=MESH)
+    pl.semaphore_wait(barrier, bands - 1)
+    finish = send_ahead(
+        range(1, bands - 1), bands, band, cell, own_ref, rest_ref, send_sem, recv_sem, 0
+    )
+    factor_steps(count, packed_ref, out_ref, work, lower, inv, diag)
+    finish()
+
+
+def factor_steps(count, packed_ref, out_ref, work, lower, inv, diag):
     size = count * BLK
     for i in range(count):
         row, col = place(i, 0, count)
@@ -465,9 +518,7 @@
 
     @pl.loop(0, count)
     def _(step):
-        tiles = invert_block(diag)
-        for t, tile in enumerate(tiles):
-            diag[t * PAN : (t + 1) * PAN, :] = tile
+        invert_block(diag)
         for j in range(count):
 
             @pl.when(step == j)
@@ -493,7 +544,7 @@
     count = size // BLK
     vmem = pl.BlockSpec(memory_space=pltpu.VMEM)
     return pl.pallas_call(
-        functools.partial(factor_kernel, count),
+        functools.partial(factor_steps, count),
         out_shape=jax.ShapeDtypeStruct((size, size), jnp.bfloat16),
         in_specs=[vmem],
         out_specs=vmem,
@@ -506,10 +557,38 @@
     )(packed)
 
 
+def inverse_and_rest(packed, own):
+    bands = lax.axis_size("band")
+    size = packed.shape[0] * 2
+    count = size // BLK
+    each = own.shape[0] // bands
+    copies = (bands - 1) * (bands - 2)
+    vmem = pl.BlockSpec(memory_space=pltpu.VMEM)
+    return pl.pallas_call(
+        functools.partial(factor_kernel, count, bands),
+        out_shape=(
+            jax.ShapeDtypeStruct((size, size), jnp.bfloat16),
+            jax.ShapeDtypeStruct((bands - 1, bands - 2, each, BLK), own.dtype),
+        ),
+        in_specs=[vmem, vmem],
+        out_specs=(vmem, vmem),
+        scratch_shapes=[
+            pltpu.VMEM((size, size), jnp.float32),
+            pltpu.VMEM((size, size), jnp.float32),
+            pltpu.VMEM((size, size), jnp.float32),
+            pltpu.VMEM((BLK, BLK), jnp.float32),
+            pltpu.SemaphoreType.DMA((copies,)),
+            pltpu.SemaphoreType.DMA((copies,)),
+        ],
+        compiler_params=pltpu.CompilerParams(collective_id=1, has_side_effects=True),
+    )(packed, own)
+
+
 def shards(wavefunctions, stiffness, cell_scale, potential):
     if fits(*wavefunctions.shape, lax.axis_size("band"), lax.axis_size("cell")):
-        slices, packed = filtered(wavefunctions, stiffness, cell_scale, potential)
-        return rotated_back(inverse_factor(packed), slices)
+        slices, own, first, packed = filtered(wavefunctions, stiffness, cell_scale, potential)
+        inverse, rest = inverse_and_rest(packed, own)
+        return rotated_here(inverse, slices, own, first, rest)
     anchor = wavefunctions.astype(jnp.float32)
     degree_one = (
         (apply_h(wavefunctions, stiffness, cell_scale, potential) - centre * anchor) / half_width

time: 96.5 us -> 87.8 us (0.910)
  Pallas kernels: 94.1 us -> 87.6 us
  local copies, waits for them, and re-layouts: 2.16 us -> 0 us
    pallas_call x2, Pallas kernels: 39.8 us -> 31.2 us  [the longest x1 27.6 us: inverse_and_rest(): pl.pallas_call(functools.partial(factor_kernel, count, bands), out_shape=...]
    unnamed x1 -> x0, local copies, waits for them, and re-layouts: 2.16 us -> none
    pallas_call x1, Pallas kernels: 54.3 us -> 56.4 us  [filtered(): pl.pallas_call(functools.partial(filter_kernel, count, bands, cells, held...]
where the time goes in v3:
time: 87.8 us; the launch traced here: 87.6 us
  Pallas kernels  87.6 us (100%)
    pallas_call x1, Pallas kernels, filtered(): pl.pallas_call(functools.partial(filter_kernel, count, bands, cells, held...  56.4 us
    pallas_call x1, Pallas kernels, inverse_and_rest(): pl.pallas_call(functools.partial(factor_kernel, count, bands), out_shape=...  27.6 us
    pallas_call x1, Pallas kernels, rotated_here(): pl.pallas_call(functools.partial(rotate_kernel, bands), out_shape=jax.Sha...  3.64 us

profile of v3, /device:TPU:0, one launch (start us, length us, event | category | flops | bytes accessed | tf_op | source)
XLA Modules:
  0.0 87.6 jit_solution(17347245142420675813)
XLA Ops:
  0.0 56.4 %shard_map.46 = (bf16[4,896,128]{2,1,0:T(8,128)(2,1)}, bf16[3584,128]{1,0:T(8,128)(2,1)}, bf16[3,1,896,128]{3,2,1,0:T(8,128)(2,1)}, f32[256,640]{1,0:T(8,128)}) custom-call(bf16[128,3584]{1,0:T(8,128)(2,1)} %wave_ref.1, bf16[512,512]{1,0:T(8,128)(2,1)} %stiff_ref.1, f32[1,8]{1,0:T(1,128)} %bitcast.1, f32[8,512]{1,0:T(8,128)} %potential_ref.1), custom_call_target="tpu_custom_call" | custom-call | tf_op jit(solution)/shard_map/pallas_call | solution.py:339
  56.4 27.6 %shard_map.47 = (bf16[512,512]{1,0:T(8,128)(2,1)}, bf16[3,2,896,128]{3,2,1,0:T(8,128)(2,1)}) custom-call(f32[256,640]{1,0:T(8,128)} %get-tuple-element.11.packed_ref, bf16[3584,128]{1,0:T(8,128)(2,1)} %get-tuple-element.12.own_ref), custom_call_target="tpu_custom_call" | custom-call | tf_op jit(solution)/shard_map/pallas_call | solution.py:567
  84.0 3.6 %shard_map.48 = bf16[128,3584]{1,0:T(8,128)(2,1)} custom-call(bf16[512,512]{1,0:T(8,128)(2,1)} %get-tuple-element.13.inverse_ref, bf16[4,896,128]{2,1,0:T(8,128)(2,1)} %get-tuple-element.14.slices_ref, bf16[3584,128]{1,0:T(8,128)(2,1)} %get-tuple-element.12.own_ref, bf16[3,1,896,128]{3,2,1,0:T(8,128)(2,1)} %get-tuple-element.15.first_ref, ...), custom_call_target="tpu_custom_call" | custom-call | tf_op jit(solution)/shard_map/pallas_call | solution.py:395

commit v4 on v3

--- a/solution.py
+++ b/solution.py
@@ -272,50 +272,83 @@
             slices_ref[i].T, joined, preferred_element_type=jnp.float32
         )
 
-    copy = send(mine.at[rows_at((1 - core) * rows_half, rows_half)], from_core, other_core)
-    copy.wait()
-    half[...] = mine[rows_at(core * rows_half, rows_half), :] + from_core[...]
-
-    copies = [
-        send(half.at[rows_at(band_peer(o) * rows_band, rows_band)], from_band.at[o - 1], band_device(o))
-        for o in range(1, bands)
-    ]
-    for copy in copies:
-        copy.wait()
-    summed = half[rows_at(band * rows_band, rows_band), :]
-    for o in range(1, bands):
-        summed = summed + from_band[o - 1]
-    quarter[...] = summed
-
-    copies = [
-        send(quarter.at[rows_at(z_peer(o) * rows_z, rows_z)], from_z.at[o - 1], z_device(o))
-        for o in range(1, levels)
-    ]
+    cuts = [0, (count + 2) // 2 * BLK, (count + 1) * BLK]
+    spans = [slice(cuts[n], cuts[n + 1]) for n in range(2)]
+    start_half = core * rows_half
+    start_band = start_half + band * rows_band
+    start_z = start_band + level * rows_z
+
+    def each_span(stage):
+        return [stage(span) for span in spans]
+
+    def wait_all(copies):
+        for copy in copies:
+            copy.wait()
+
+    over_core = each_span(
+        lambda span: [
+            send(
+                mine.at[rows_at((1 - core) * rows_half, rows_half), span],
+                from_core.at[:, span],
+                other_core,
+            )
+        ]
+    )
+    over_band = []
+    for span, copies in zip(spans, over_core):
+        wait_all(copies)
+        half[:, span] = mine[rows_at(start_half, rows_half), span] + from_core[:, span]
+        over_band.append([
+            send(
+                half.at[rows_at(band_peer(o) * rows_band, rows_band), span],
+                from_band.at[o - 1, :, span],
+                band_device(o),
+            )
+            for o in range(1, bands)
+        ])
+    over_z = []
+    for span, copies in zip(spans, over_band):
+        wait_all(copies)
+        summed = half[rows_at(band * rows_band, rows_band), span]
+        for o in range(1, bands):
+            summed = summed + from_band[o - 1, :, span]
+        quarter[:, span] = summed
+        over_z.append([
+            send(
+                quarter.at[rows_at(z_peer(o) * rows_z, rows_z), span],
+                from_z.at[o - 1, :, span],
+                z_device(o),
+            )
+            for o in range(1, levels)
+        ])
     finish_ahead = send_ahead(
         range(0, 1), bands, band, cell, three, ahead_ref, send_sem, recv_sem, send_sem.shape[0] - bands + 1
     )
-    for copy in copies:
-        copy.wait()
-    summed = quarter[rows_at(level * rows_z, rows_z), :]
-    for o in range(1, levels):
-        summed = summed + from_z[o - 1]
-    summed = summed / total
-    piece[...] = summed
-
-    start_half = core * rows_half
-    start_band = start_half + band * rows_band
-    start_z = start_band + level * rows_z
-    here = rows_at(start_z, rows_z)
-    out_ref[here, :] = summed
-    copies = [send(piece, out_ref.at[here], z_device(o)) for o in range(1, levels)]
-    for copy in copies:
-        copy.wait()
-    here = out_ref.at[rows_at(start_band, rows_band)]
-    copies = [send(here, here, band_device(o)) for o in range(1, bands)]
-    for copy in copies:
-        copy.wait()
-    here = out_ref.at[rows_at(start_half, rows_half)]
-    send(here, here, other_core).wait()
+    back_z = []
+    for span, copies in zip(spans, over_z):
+        wait_all(copies)
+        summed = quarter[rows_at(level * rows_z, rows_z), span]
+        for o in range(1, levels):
+            summed = summed + from_z[o - 1, :, span]
+        summed = summed / total
+        piece[:, span] = summed
+        here = rows_at(start_z, rows_z)
+        out_ref[here, span] = summed
+        back_z.append([
+            send(piece.at[:, span], out_ref.at[here, span], z_device(o)) for o in range(1, levels)
+        ])
+    back_band = []
+    for span, copies in zip(spans, back_z):
+        wait_all(copies)
+        here = out_ref.at[rows_at(start_band, rows_band), span]
+        back_band.append([send(here, here, band_device(o)) for o in range(1, bands)])
+    back_core = []
+    for span, copies in zip(spans, back_band):
+        wait_all(copies)
+        here = out_ref.at[rows_at(start_half, rows_half), span]
+        back_core.append([send(here, here, other_core)])
+    for copies in back_core:
+        wait_all(copies)
     finish_ahead()
 
 
@@ -332,7 +365,7 @@
     rows_half = height // 2
     rows_band = rows_half // bands
     rows_z = rows_band // levels
-    sends = 4 + 2 * (bands - 1) + 2 * (1 + (bands - 1) + (levels - 1))
+    sends = 4 + 2 * (bands - 1) + 4 * (1 + (bands - 1) + (levels - 1))
     spans = owned + 5 * OWN + PLANE
     vmem = pl.BlockSpec(memory_space=pltpu.VMEM)
     f32, bf16 = jnp.float32, jnp.bfloat16
@@ -514,27 +547,27 @@
         width = (i + 1) * BLK
         work[i * BLK : (i + 1) * BLK, :width] = packed_ref[row : row + BLK, col : col + width]
     inv[...] = jnp.zeros_like(inv)
-    diag[...] = work[:BLK, :BLK]
-
-    @pl.loop(0, count)
-    def _(step):
-        invert_block(diag)
-        for j in range(count):
-
-            @pl.when(step == j)
-            def _():
-                here = slice(j * BLK, (j + 1) * BLK)
-                top = diag[...]
-                if j:
-                    partial = exact(lower[here, : j * BLK], inv[: j * BLK, : j * BLK], NN)
-                    inv[here, : j * BLK] = -exact(top, partial, NN)
-                inv[here, here] = top
-                if j + 1 < count:
-                    below = slice((j + 1) * BLK, size)
-                    panel = exact(work[below, here], top, NT)
-                    lower[below, here] = panel
-                    work[below, below] = work[below, below] - exact(panel, panel, NT)
-                    diag[...] = work[(j + 1) * BLK : (j + 2) * BLK, (j + 1) * BLK : (j + 2) * BLK]
+    block = lambda i: slice(i * BLK, (i + 1) * BLK)
+    diag[0] = work[:BLK, :BLK]
+    invert_block(diag.at[0])
+    for j in range(count):
+        here, top = block(j), diag[j]
+        if j + 1 < count:
+            ahead = block(j + 1)
+            panel = exact(work[ahead, here], top, NT)
+            lower[ahead, here] = panel
+            diag[j + 1] = work[ahead, ahead] - exact(panel, panel, NT)
+            invert_block(diag.at[j + 1])
+            for i in range(j + 2, count):
+                lower[block(i), here] = exact(work[block(i), here], top, NT)
+                for q in range(j + 1, i + 1):
+                    work[block(i), block(q)] = work[block(i), block(q)] - exact(
+                        lower[block(i), here], lower[block(q), here], NT
+                    )
+        if j:
+            partial = exact(lower[here, : j * BLK], inv[: j * BLK, : j * BLK], NN)
+            inv[here, : j * BLK] = -exact(top, partial, NN)
+        inv[here, here] = top
 
     out_ref[...] = inv[...].astype(out_ref.dtype)
 
@@ -552,7 +585,7 @@
             pltpu.VMEM((size, size), jnp.float32),
             pltpu.VMEM((size, size), jnp.float32),
             pltpu.VMEM((size, size), jnp.float32),
-            pltpu.VMEM((BLK, BLK), jnp.float32),
+            pltpu.VMEM((count, BLK, BLK), jnp.float32),
         ],
     )(packed)
 
@@ -576,7 +609,7 @@
             pltpu.VMEM((size, size), jnp.float32),
             pltpu.VMEM((size, size), jnp.float32),
             pltpu.VMEM((size, size), jnp.float32),
-            pltpu.VMEM((BLK, BLK), jnp.float32),
+            pltpu.VMEM((count, BLK, BLK), jnp.float32),
             pltpu.SemaphoreType.DMA((copies,)),
             pltpu.SemaphoreType.DMA((copies,)),
         ],

time: 87.8 us -> 87.8 us (level)
  no operation moved by 1% of the time
where the time goes in v4:
time: 87.8 us; the launch traced here: 87.6 us
  Pallas kernels  87.6 us (100%)
    pallas_call x1, Pallas kernels, filtered(): pl.pallas_call(functools.partial(filter_kernel, count, bands, cells, held...  56.1 us
    pallas_call x1, Pallas kernels, inverse_and_rest(): pl.pallas_call(functools.partial(factor_kernel, count, bands), out_shape=...  27.8 us
    pallas_call x1, Pallas kernels, rotated_here(): pl.pallas_call(functools.partial(rotate_kernel, bands), out_shape=jax.Sha...  3.64 us

profile of v4, /device:TPU:0, one launch (start us, length us, event | category | flops | bytes accessed | tf_op | source)
XLA Modules:
  0.0 87.6 jit_solution(4182412591722660455)
XLA Ops:
  0.0 56.1 %shard_map.46 = (bf16[4,896,128]{2,1,0:T(8,128)(2,1)}, bf16[3584,128]{1,0:T(8,128)(2,1)}, bf16[3,1,896,128]{3,2,1,0:T(8,128)(2,1)}, f32[256,640]{1,0:T(8,128)}) custom-call(bf16[128,3584]{1,0:T(8,128)(2,1)} %wave_ref.1, bf16[512,512]{1,0:T(8,128)(2,1)} %stiff_ref.1, f32[1,8]{1,0:T(1,128)} %bitcast.1, f32[8,512]{1,0:T(8,128)} %potential_ref.1), custom_call_target="tpu_custom_call" | custom-call | tf_op jit(solution)/shard_map/pallas_call | solution.py:372
  56.1 27.8 %shard_map.47 = (bf16[512,512]{1,0:T(8,128)(2,1)}, bf16[3,2,896,128]{3,2,1,0:T(8,128)(2,1)}) custom-call(f32[256,640]{1,0:T(8,128)} %get-tuple-element.11.packed_ref, bf16[3584,128]{1,0:T(8,128)(2,1)} %get-tuple-element.12.own_ref), custom_call_target="tpu_custom_call" | custom-call | tf_op jit(solution)/shard_map/pallas_call | solution.py:600
  84.0 3.6 %shard_map.48 = bf16[128,3584]{1,0:T(8,128)(2,1)} custom-call(bf16[512,512]{1,0:T(8,128)(2,1)} %get-tuple-element.13.inverse_ref, bf16[4,896,128]{2,1,0:T(8,128)(2,1)} %get-tuple-element.14.slices_ref, bf16[3584,128]{1,0:T(8,128)(2,1)} %get-tuple-element.12.own_ref, bf16[3,1,896,128]{3,2,1,0:T(8,128)(2,1)} %get-tuple-element.15.first_ref, ...), custom_call_target="tpu_custom_call" | custom-call | tf_op jit(solution)/shard_map/pallas_call | solution.py:428

commit v5 on v4

--- a/solution.py
+++ b/solution.py
@@ -263,6 +263,9 @@
             slices_ref[band] = piece_of[...]
     for copy in swaps:
         copy.wait()
+    finish_ahead = send_ahead(
+        range(0, 1), bands, band, cell, three, ahead_ref, send_sem, recv_sem, send_sem.shape[0] - bands + 1
+    )
 
     for i in range(count):
         row, col = place(i, 0, count)
@@ -321,9 +324,6 @@
             )
             for o in range(1, levels)
         ])
-    finish_ahead = send_ahead(
-        range(0, 1), bands, band, cell, three, ahead_ref, send_sem, recv_sem, send_sem.shape[0] - bands + 1
-    )
     back_z = []
     for span, copies in zip(spans, over_z):
         wait_all(copies)

time: 87.8 us -> 91.2 us (1.039)
  Pallas kernels: 87.6 us -> 91 us
    pallas_call x1, Pallas kernels: 56.1 us -> 61.8 us  [filtered(): pl.pallas_call(functools.partial(filter_kernel, count, bands, cells, held...]
    pallas_call x1, Pallas kernels: 27.8 us -> 25.5 us  [inverse_and_rest(): pl.pallas_call(functools.partial(factor_kernel, count, bands), out_shape=...]
where the time goes in v5:
time: 91.2 us; the launch traced here: 91 us
  Pallas kernels  91 us (100%)
    pallas_call x1, Pallas kernels, filtered(): pl.pallas_call(functools.partial(filter_kernel, count, bands, cells, held...  61.8 us
    pallas_call x1, Pallas kernels, inverse_and_rest(): pl.pallas_call(functools.partial(factor_kernel, count, bands), out_shape=...  25.5 us
    pallas_call x1, Pallas kernels, rotated_here(): pl.pallas_call(functools.partial(rotate_kernel, bands), out_shape=jax.Sha...  3.64 us

profile of v5, /device:TPU:0, one launch (start us, length us, event | category | flops | bytes accessed | tf_op | source)
XLA Modules:
  0.0 91.0 jit_solution(2551314607216598378)
XLA Ops:
  0.0 61.8 %shard_map.46 = (bf16[4,896,128]{2,1,0:T(8,128)(2,1)}, bf16[3584,128]{1,0:T(8,128)(2,1)}, bf16[3,1,896,128]{3,2,1,0:T(8,128)(2,1)}, f32[256,640]{1,0:T(8,128)}) custom-call(bf16[128,3584]{1,0:T(8,128)(2,1)} %wave_ref.1, bf16[512,512]{1,0:T(8,128)(2,1)} %stiff_ref.1, f32[1,8]{1,0:T(1,128)} %bitcast.1, f32[8,512]{1,0:T(8,128)} %potential_ref.1), custom_call_target="tpu_custom_call" | custom-call | tf_op jit(solution)/shard_map/pallas_call | solution.py:372
  61.8 25.5 %shard_map.47 = (bf16[512,512]{1,0:T(8,128)(2,1)}, bf16[3,2,896,128]{3,2,1,0:T(8,128)(2,1)}) custom-call(f32[256,640]{1,0:T(8,128)} %get-tuple-element.11.packed_ref, bf16[3584,128]{1,0:T(8,128)(2,1)} %get-tuple-element.12.own_ref), custom_call_target="tpu_custom_call" | custom-call | tf_op jit(solution)/shard_map/pallas_call | solution.py:600
  87.4 3.6 %shard_map.48 = bf16[128,3584]{1,0:T(8,128)(2,1)} custom-call(bf16[512,512]{1,0:T(8,128)(2,1)} %get-tuple-element.13.inverse_ref, bf16[4,896,128]{2,1,0:T(8,128)(2,1)} %get-tuple-element.14.slices_ref, bf16[3584,128]{1,0:T(8,128)(2,1)} %get-tuple-element.12.own_ref, bf16[3,1,896,128]{3,2,1,0:T(8,128)(2,1)} %get-tuple-element.15.first_ref, ...), custom_call_target="tpu_custom_call" | custom-call | tf_op jit(solution)/shard_map/pallas_call | solution.py:428
